TPU v7x, 32 devices: a whole 2x2x4 slice. The times are simulated.
32 devices in a mesh: segment: 2 (over y), expert: 16 (over z, x, core).
Axes of the slice: x: 2, y: 2, z: 4, core: 2. Of those that a mesh axis runs over, the one named last changes fastest.
Arguments:
- hidden: bfloat16 [2, 512, 2048], P('segment', 'expert'), may hold values from -6 to 6
- memory: bfloat16 [2, 512, 2048], P('segment', 'expert'), may hold values from -6 to 6
- lengths: int32 [2, 16], P('segment', 'expert'), may hold values from 1 to 32, as said below
- memory_lengths: int32 [2, 16], P('segment', 'expert'), may hold values from 1 to 32, as said below
- routes: int32 [2, 512, 2], P('segment', 'expert'), may hold values from 0 to 3, all different within a row; in each aligned block of 32 rows (0 to 31, 32 to 63, ..., all dimensions but the last counted through in order) at most 20 rows name the same one
- norm_gain: float32 [2, 3, 2048], P('segment'), may hold values from 0.5 to 1.5, as said below
- router: bfloat16 [2, 2048, 4], P('segment'), may hold values from -0.26516504 to 0.26516504, as said below
- w_in: bfloat16 [2, 2048, 16384], P('segment', None, 'expert'), may hold values from -0.13258252 to 0.13258252, as said below
- w_out: bfloat16 [2, 16384, 2048], P('segment', 'expert'), may hold values from -0.125 to 0.125, as said below
- shortlist: bfloat16 [2, 2048, 512], P('segment'), may hold values from -0.375 to 0.375
- student: float32 [2, 512, 512], P('segment', 'expert'), may hold values from -15 to 15
- targets: int32 [2, 512], P('segment', 'expert'), may hold values from 0 to 511
Outputs:
- layer_out: bfloat16 [2, 512, 2048], P('segment', 'expert')
- loss: float32 [], replicated
Inputs may be any that keep to these rules, and one draw needn't show every extreme that they name: `lengths`: every sequence has at least one position; the first sequence of each section has 32. `memory_lengths`: every sequence has at least one position; the first sequence of each section has 32. `routes`: A token's two experts differ. In the 32 rows of one device no expert is named more than 20 times, a bound that some block reaches. `norm_gain`: equal in all encoder sections, and equal in all decoder sections. `router`: equal in all encoder sections, and equal in all decoder sections. `w_in`: equal in all encoder sections, and equal in all decoder sections. `w_out`: equal in all encoder sections, and equal in all decoder sections.
All inputs are finite; a program needn't handle non-finite values.
Results may differ from a plain program's by a relative error of at most 0.0049.
Values may be sent and summed in bfloat16 or wider, within the bound.
A program may use at most 64 MiB of HBM per device.

v0:
```python
import functools
import math

import jax
import jax.numpy as jnp
from jax import lax
from jax.experimental import pallas as pl
from jax.experimental.pallas import tpu as pltpu
from jax.sharding import PartitionSpec as P

HEAD_DIM = 128
LEN = 32
EPS = 1e-05
MESH = pl.DeviceIdType.MESH
BF = jnp.bfloat16
F32 = jnp.float32


def layer_norm(values, gain_row):
    centred = values - jnp.mean(values, axis=-1, keepdims=True)
    spread = jnp.mean(centred * centred, axis=-1, keepdims=True)
    return centred * lax.rsqrt(spread + EPS) * gain_row


def xor(a, k, count):
    out = 0
    bit = 1
    while bit < count:
        out = out + lax.rem(a // bit + (k // bit) % 2, 2) * bit
        bit *= 2
    return out


def kernel(
    n_seg, n_exp, experts, gx, gc,
    hidden_any, memory, lengths, memory_lengths, routes_any, gain_any, router_any,
    w_in, w_out, shortlist, student_any, targets,
    layer_out, loss_out,
    hidden, routes, norm_gain, router, student, out_stage,
    win, wout, short, kmem, klen_src, klen, mid,
    out_a, out_b, x, x_b, stage, act, y0,
    core_a, core_b, rc_a, rc_b, xs_a, xs_b, rx_a, rx_b, zs_a, zs_b, z_a, z_b, z_all, z_stage,
    lsend, lrecv,
    wsem, msem, ra, sz, sx, sc, rc_s, rc_r, rx_s, rx_r, rz_s, rz_r, l_s, l_r,
):
    seg = lax.axis_index("segment")
    me = lax.axis_index("expert")
    half_seg = n_seg // 2
    group = gx * gc
    e = me // group
    j = lax.rem(me, group)
    xi = j // gc
    ci = lax.rem(j, gc)
    tok = hidden.shape[1]
    width = hidden.shape[2]
    heads = width // HEAD_DIM
    cap = 5 * tok // 8
    main = cap // 16 * 16
    rest = cap - main
    hop_order = [k for k in range(experts // 2, experts)] + [k for k in range(1, experts // 2)]

    def peer(ds, d):
        return (lax.rem(seg + ds, n_seg), lax.rem(me + d, n_exp))

    def dev(e2, x2, c2):
        return (seg, (e2 * gx + x2) * gc + c2)

    barrier = pltpu.get_barrier_semaphore()
    for ds in range(n_seg):
        for d in range(n_exp):
            if ds or d:
                pl.semaphore_signal(
                    barrier, inc=1, device_id=peer(ds, d), device_id_type=MESH
                )

    early = [
        pltpu.make_async_copy(hidden_any, hidden, wsem.at[3]),
        pltpu.make_async_copy(gain_any, norm_gain, wsem.at[4]),
        pltpu.make_async_copy(routes_any, routes, wsem.at[5]),
        pltpu.make_async_copy(router_any, router, wsem.at[6]),
        pltpu.make_async_copy(student_any, student, wsem.at[7]),
    ]
    for load in early:
        load.start()
    loads = [
        pltpu.make_async_copy(w_in.at[0], win, wsem.at[0]),
        pltpu.make_async_copy(w_out.at[0], wout, wsem.at[1]),
        pltpu.make_async_copy(shortlist.at[0], short, wsem.at[2]),
    ]
    for load in loads:
        load.start()

    klen_src[...] = jnp.broadcast_to(memory_lengths[0:1, 0:1], klen_src.shape)
    for q in range(1, tok // LEN):
        klen_src[q : q + 1, :] = jnp.broadcast_to(memory_lengths[0:1, q : q + 1], (1, 128))
    early[0].wait()
    early[1].wait()
    gains = [norm_gain[i] for i in range(3)]
    states = hidden[0].astype(F32)
    pl.semaphore_wait(barrier, n_exp * n_seg - 1)

    is_decoder = seg >= half_seg
    to_seg = lax.rem(seg + half_seg, n_seg)
    mem_copy = pltpu.make_async_remote_copy(
        memory.at[0], kmem, msem.at[0], msem.at[1], device_id=(to_seg, me), device_id_type=MESH
    )
    len_copy = pltpu.make_async_remote_copy(
        klen_src, klen, msem.at[2], msem.at[3], device_id=(to_seg, me), device_id_type=MESH
    )

    @pl.when(seg < half_seg)
    def _():
        mem_copy.start()
        len_copy.start()
        mid[...] = states

    @pl.when(seg >= half_seg)
    def _():
        queries = layer_norm(states, gains[0]).astype(BF)
        len_copy.wait_recv()
        mem_copy.wait_recv()
        keys = kmem[...]
        col = lax.broadcasted_iota(jnp.int32, (tok, tok), 1)
        row = lax.broadcasted_iota(jnp.int32, (tok, tok), 0)
        klen_v = klen[...]
        allowed = jnp.zeros((tok, tok), jnp.bool_)
        for q in range(tok // LEN):
            inside = (col >= q * LEN) & (col - q * LEN < klen_v[q : q + 1, 0:1])
            inside = inside & (col < (q + 1) * LEN) & (row >= q * LEN) & (row < (q + 1) * LEN)
            allowed = allowed | inside
        scores = jnp.concatenate(
            [
                jnp.where(
                    allowed,
                    lax.dot_general(
                        queries[:, h * HEAD_DIM : (h + 1) * HEAD_DIM],
                        keys[:, h * HEAD_DIM : (h + 1) * HEAD_DIM],
                        (((1,), (1,)), ((), ())),
                        preferred_element_type=F32,
                    )
                    * (1.0 / math.sqrt(HEAD_DIM)),
                    -1e30,
                )
                for h in range(heads)
            ],
            axis=0,
        )
        top = jnp.max(scores, axis=-1, keepdims=True)
        raised = jnp.exp(scores - top)
        weights = (raised / jnp.sum(raised, axis=-1, keepdims=True)).astype(BF)
        for h in range(heads):
            part = slice(h * HEAD_DIM, (h + 1) * HEAD_DIM)
            mid[:, part] = states[:, part] + jnp.dot(
                weights[h * tok : (h + 1) * tok], keys[:, part], preferred_element_type=F32
            )

    normed = layer_norm(mid[...], gains[1]).astype(BF)

    early[2].wait()
    expert_lane = lax.broadcasted_iota(jnp.int32, (tok, experts), 1)
    pos = lax.broadcasted_iota(jnp.int32, (tok, 1), 0)
    valid = jnp.zeros((tok, 1), F32)
    for q in range(tok // LEN):
        ok = (pos >= q * LEN) & (pos < (q + 1) * LEN) & (pos - q * LEN < lengths[0:1, q : q + 1])
        valid = valid + ok.astype(F32)
    square = lax.broadcasted_iota(jnp.int32, (tok, tok), 0) == lax.broadcasted_iota(
        jnp.int32, (tok, tok), 1
    )

    def column(row):
        spread = jnp.where(square, jnp.broadcast_to(row, (tok, tok)), 0)
        return jnp.sum(spread.astype(F32), axis=-1, keepdims=True)

    expert_lane = expert_lane.astype(F32)
    first_hot = (column(routes[0, 0:1, :]) == expert_lane).astype(F32)
    second_hot = (column(routes[0, 1:2, :]) == expert_lane).astype(F32)
    chosen = (first_hot + second_hot) * valid
    before = (
        lax.broadcasted_iota(jnp.int32, (tok, tok), 1)
        < lax.broadcasted_iota(jnp.int32, (tok, tok), 0)
    ).astype(BF)
    rank = jnp.dot(before, chosen.astype(BF), preferred_element_type=F32)
    n_main = experts * main
    n_slots = experts * cap
    lanes = -(-n_slots // 128) * 128
    lane = lax.broadcasted_iota(jnp.int32, (1, lanes), 1)
    slot_of = jnp.full((1, lanes), -1, jnp.int32)
    expert_of = jnp.full((1, lanes), -1, jnp.int32)
    for k in range(experts):
        ek = xor(e, k, experts)
        in_main = (lane >= k * main) & (lane < (k + 1) * main)
        low = n_main + k * rest
        in_rest = (lane >= low) & (lane < low + rest)
        slot_of = jnp.where(in_main, lane - k * main, slot_of)
        slot_of = jnp.where(in_rest, lane - low + main, slot_of)
        expert_of = jnp.where(in_main | in_rest, ek, expert_of)
    placing = jnp.zeros((tok, lanes), F32)
    for k in range(experts):
        here = (expert_of == k) & (rank[:, k : k + 1] == slot_of.astype(F32))
        placing = placing + jnp.where(here, chosen[:, k : k + 1], 0.0)
    place_rows = jnp.transpose(placing)[0:n_slots].astype(BF)
    slots = jnp.dot(place_rows, normed, preferred_element_type=F32)

    def rows_a(dc, dx, k):
        return pl.ds(dc * gx * experts * cap + (dx * experts + k) * main, main)

    def index_b(dc, dx, k):
        return (dc * gx + dx) * experts + k

    x[rows_a(0, 0, 0), :] = slots[0:main].astype(BF)
    x_b[0] = slots[n_main : n_main + rest].astype(BF)
    for k in hop_order:
        out_a[k] = slots[k * main : (k + 1) * main].astype(BF)
        out_b[k] = slots[n_main + k * rest : n_main + (k + 1) * rest].astype(BF)

    waits = []

    def send(src, dst, s_sem, r_sem, target):
        copy = pltpu.make_async_remote_copy(
            src, dst, s_sem, r_sem, device_id=target, device_id_type=MESH
        )
        copy.start()
        waits.append(copy)

    def landed(ref, sem):
        pltpu.make_async_copy(ref, ref, sem).wait()

    half_width = width // 2

    def piece(slot, p):
        if p < 2:
            return x.at[rows_a(*slot), p * half_width : (p + 1) * half_width]
        return x_b.at[index_b(*slot)]

    def arrived(slot, p):
        landed(piece(slot, p), ra.at[3 * index_b(*slot) + p])

    def forward(slot_from, slot_to, p, sems, base, target):
        send(
            piece(slot_from, p), piece(slot_to, p), sems.at[3 * base + p],
            ra.at[3 * index_b(*slot_to) + p], target,
        )

    for k in hop_order:
        target = dev(xor(e, k, experts), xi, ci)
        for p in range(3):
            src = out_a.at[k, :, p * half_width : (p + 1) * half_width] if p < 2 else out_b.at[k]
            send(
                src, piece((0, 0, k), p), sz.at[3 * k + p], ra.at[3 * index_b(0, 0, k) + p], target
            )

    core_dev = dev(e, xi, lax.rem(ci + 1, gc))

    def from_column(k):
        for p in range(3):
            if k:
                arrived((0, 0, k), p)
            for d in range(1, gx):
                forward(
                    (0, 0, k), (0, d, k), p, sx, (d - 1) * experts + k,
                    dev(e, lax.rem(xi + d, gx), ci),
                )
            forward((0, 0, k), (1, 0, k), p, sc, k, core_dev)

    def from_chips(k):
        for p in range(3):
            for d in range(1, gx):
                arrived((0, d, k), p)
                forward((0, d, k), (1, d, k), p, sc, d * experts + k, core_dev)

    order = [0] + hop_order
    for i, k in enumerate(order):
        from_column(k)
        if i:
            from_chips(order[i - 1])
    from_chips(order[-1])
    for k in order:
        for d in range(gx):
            for p in range(3):
                arrived((1, d, k), p)

    blocks = gx * experts
    half_rows = blocks * cap
    half_main = blocks * main
    for dc in range(gc):
        for i in range(blocks):
            stage[i * rest : (i + 1) * rest, :] = x_b[dc * blocks + i].astype(F32)
        x[dc * half_rows + half_main : (dc + 1) * half_rows, :] = stage[...].astype(BF)

    units = win.shape[1]
    tile = min(256, units)
    loads[0].wait()

    @pl.loop(0, units // tile)
    def _(i):
        cols = pl.ds(pl.multiple_of(i * tile, tile), tile)
        act[:, cols] = jnp.maximum(
            jnp.dot(x[...], win[:, cols], preferred_element_type=F32), 0.0
        ).astype(BF)

    loads[1].wait()
    tile2 = 256

    @pl.loop(0, width // tile2)
    def _(i):
        cols = pl.ds(pl.multiple_of(i * tile2, tile2), tile2)
        part = jnp.dot(act[half_rows:, :], wout[:, cols], preferred_element_type=F32)
        core_a[:, cols] = part[0:half_main].astype(BF)
        for b in range(blocks):
            core_b[b, :, cols] = part[half_main + b * rest : half_main + (b + 1) * rest].astype(BF)

    send(core_a, rc_a, rc_s.at[0], rc_r.at[0], core_dev)
    send(core_b, rc_b, rc_s.at[1], rc_r.at[1], core_dev)

    @pl.loop(0, width // tile2)
    def _(i):
        cols = pl.ds(pl.multiple_of(i * tile2, tile2), tile2)
        y0[:, cols] = jnp.dot(act[0:half_rows, :], wout[:, cols], preferred_element_type=F32)

    landed(rc_a, rc_r.at[0])
    landed(rc_b, rc_r.at[1])

    def chip_sum(dx, k):
        b = dx * experts + k
        sum_a = y0[b * main : (b + 1) * main, :] + rc_a[b * main : (b + 1) * main, :].astype(F32)
        low = half_main + b * rest
        sum_b = y0[low : low + rest, :] + rc_b[b].astype(F32)
        return sum_a, sum_b

    back_order = hop_order + [0]
    for k in back_order:
        for d in range(1, gx):
            o = (d - 1) * experts + k
            sum_a, sum_b = chip_sum(d, k)
            xs_a[o] = sum_a.astype(BF)
            xs_b[o] = sum_b.astype(BF)
            target = dev(e, lax.rem(xi + gx - d, gx), ci)
            send(xs_a.at[o], rx_a.at[o], rx_s.at[2 * o], rx_r.at[2 * o], target)
            send(xs_b.at[o], rx_b.at[o], rx_s.at[2 * o + 1], rx_r.at[2 * o + 1], target)
    for k in back_order:
        sum_a, sum_b = chip_sum(0, k)
        for d in range(1, gx):
            o = (d - 1) * experts + k
            landed(rx_a.at[o], rx_r.at[2 * o])
            landed(rx_b.at[o], rx_r.at[2 * o + 1])
            sum_a = sum_a + rx_a[o].astype(F32)
            sum_b = sum_b + rx_b[o].astype(F32)
        if k:
            zs_a[k] = sum_a.astype(BF)
            zs_b[k] = sum_b.astype(BF)
            target = dev(xor(e, k, experts), xi, ci)
            send(zs_a.at[k], z_a.at[k], rz_s.at[2 * k], rz_r.at[2 * k], target)
            send(zs_b.at[k], z_b.at[k], rz_s.at[2 * k + 1], rz_r.at[2 * k + 1], target)
        else:
            z_all[0:main, :] = sum_a.astype(BF)
            z_stage[0:rest, :] = sum_b

    early[3].wait()
    probs = lax.dot_general(
        normed, router[0], (((1,), (1,)), ((), ())), preferred_element_type=F32
    )
    probs = jnp.exp(probs - jnp.max(probs, axis=-1, keepdims=True))
    probs = probs / jnp.sum(probs, axis=-1, keepdims=True)
    prob_first = jnp.sum(probs * first_hot, axis=-1, keepdims=True)
    prob_second = jnp.sum(probs * second_hot, axis=-1, keepdims=True)
    gate = (prob_first * first_hot + prob_second * second_hot) / (prob_first + prob_second)
    combine = jnp.zeros((tok, lanes), F32)
    for k in range(experts):
        combine = combine + jnp.where(expert_of == k, gate[:, k : k + 1], 0.0)
    combine = (combine * placing)[:, 0:n_slots]
    high = combine.astype(BF)
    low = (combine - high.astype(F32)).astype(BF)

    early[4].wait()
    learner_in = student[0]
    shifted = learner_in - jnp.max(learner_in, axis=-1, keepdims=True)
    learner = shifted - jnp.log(jnp.sum(jnp.exp(shifted), axis=-1, keepdims=True))
    target_col = column(targets[0:1, :])
    vocab = student.shape[2]
    picked = lax.broadcasted_iota(jnp.int32, (tok, vocab), 1).astype(F32) == target_col
    hit = jnp.sum(jnp.where(picked, learner, 0.0), axis=-1, keepdims=True)
    loads[2].wait()

    for k in hop_order:
        landed(z_a.at[k], rz_r.at[2 * k])
        landed(z_b.at[k], rz_r.at[2 * k + 1])
        z_all[k * main : (k + 1) * main, :] = z_a[k]
        z_stage[k * rest : (k + 1) * rest, :] = z_b[k].astype(F32)
    z_all[n_main:, :] = z_stage[...].astype(BF)
    back = z_all[...]
    moe = jnp.dot(high, back, preferred_element_type=F32) + jnp.dot(
        low, back, preferred_element_type=F32
    )
    out = (mid[...] + moe).astype(BF)
    out_stage[...] = out
    out_copy = pltpu.make_async_copy(out_stage, layer_out.at[0], wsem.at[8])
    out_copy.start()

    final = layer_norm(out.astype(F32), gains[2]).astype(BF)
    logits = jnp.dot(final, short[...], preferred_element_type=F32)
    logits = logits - jnp.max(logits, axis=-1, keepdims=True)
    teacher = logits - jnp.log(jnp.sum(jnp.exp(logits), axis=-1, keepdims=True))
    token_loss = jnp.sum(jnp.exp(teacher) * (teacher - learner), axis=-1, keepdims=True) - hit
    counted = jnp.where(is_decoder, valid, 0.0)
    loss_sum = jnp.sum(token_loss * counted, axis=0, keepdims=True)
    loss_count = jnp.sum(counted, axis=0, keepdims=True)
    spot = lax.broadcasted_iota(jnp.int32, lsend.shape, 1)
    pair = jnp.where(spot == 0, loss_sum, jnp.where(spot == 1, loss_count, 0.0))
    lsend[...] = pair

    @pl.when(is_decoder)
    def _():
        mine = (seg - half_seg) * n_exp
        lrecv[mine + me] = pair
        for ds in range(n_seg):
            for d in range(n_exp):
                if ds or d:
                    pltpu.make_async_remote_copy(
                        lsend, lrecv.at[mine + me], l_s.at[ds * n_exp + d], l_r.at[mine + d],
                        device_id=peer(ds, d), device_id_type=MESH,
                    ).start()

    for q in range(n_seg - half_seg):
        for d in range(n_exp):
            source = q * n_exp + lax.rem(me + n_exp - d, n_exp)
            if d:
                landed(lrecv.at[source], l_r.at[q * n_exp + d])
            else:
                @pl.when(seg != q + half_seg)
                def _():
                    landed(lrecv.at[source], l_r.at[q * n_exp])

    total = lrecv[0]
    for i in range(1, (n_seg - half_seg) * n_exp):
        total = total + lrecv[i]
    loss_out[...] = total[0:1, 0:1] / total[0:1, 1:2]

    @pl.when(is_decoder)
    def _():
        for i in range(1, n_seg * n_exp):
            pltpu.make_async_copy(lsend, lsend, l_s.at[i]).wait()

    out_copy.wait()
    for copy in waits:
        copy.wait_send()

    @pl.when(seg < half_seg)
    def _():
        mem_copy.wait_send()
        len_copy.wait_send()


def local(
    hidden, memory, lengths, memory_lengths, routes, norm_gain, router,
    w_in, w_out, shortlist, student, targets,
):
    n_seg = lax.axis_size("segment")
    n_exp = lax.axis_size("expert")
    experts = router.shape[2]
    group = n_exp // experts
    gc = 2
    gx = group // gc
    tok, width = hidden.shape[1], hidden.shape[2]
    units = w_in.shape[2]
    vocab = shortlist.shape[2]
    cap = 5 * tok // 8
    main = cap // 16 * 16
    rest = cap - main
    blocks = gx * experts
    half_rows = blocks * cap
    vm = pl.BlockSpec(memory_space=pltpu.VMEM)
    hbm = pl.BlockSpec(memory_space=pl.ANY)
    v = pltpu.VMEM
    dma = pltpu.SemaphoreType.DMA
    nx = max(gx - 1, 1) * experts
    scratch = [
        v((1, tok, width), BF), v((1, 2, tok), jnp.int32), v((3, 1, width), F32),
        v((1, experts, width), BF), v((1, tok, vocab), F32), v((tok, width), BF),
        v((width, units), BF), v((units, width), BF), v((width, vocab), BF),
        v((tok, width), BF), v((8, 128), jnp.int32), v((8, 128), jnp.int32), v((tok, width), F32),
        v((experts, main, width), BF), v((experts, rest, width), BF),
        v((gc * half_rows, width), BF), v((gc * blocks, rest, width), BF),
        v((blocks * rest, width), F32), v((gc * half_rows, units), BF), v((half_rows, width), F32),
        v((blocks * main, width), BF), v((blocks, rest, width), BF),
        v((blocks * main, width), BF), v((blocks, rest, width), BF),
        v((nx, main, width), BF), v((nx, rest, width), BF),
        v((nx, main, width), BF), v((nx, rest, width), BF),
        v((experts, main, width), BF), v((experts, rest, width), BF),
        v((experts, main, width), BF), v((experts, rest, width), BF),
        v((experts * cap, width), BF), v((experts * rest, width), F32),
        v((8, 128), F32), v(((n_seg - n_seg // 2) * n_exp, 8, 128), F32),
        dma((9,)), dma((4,)), dma((3 * gc * blocks,)),
        dma((3 * experts,)), dma((3 * nx,)), dma((3 * blocks,)),
        dma((2,)), dma((2,)), dma((2 * nx,)), dma((2 * nx,)),
        dma((2 * experts,)), dma((2 * experts,)),
        dma((n_seg * n_exp,)), dma(((n_seg - n_seg // 2) * n_exp,)),
    ]
    layer_out, loss = pl.pallas_call(
        functools.partial(kernel, n_seg, n_exp, experts, gx, gc),
        out_shape=(
            jax.ShapeDtypeStruct((1, tok, width), BF),
            jax.ShapeDtypeStruct((1, 1), F32),
        ),
        in_specs=[hbm, hbm, vm, vm, hbm, hbm, hbm, hbm, hbm, hbm, hbm, vm],
        out_specs=(hbm, vm),
        scratch_shapes=scratch,
        compiler_params=pltpu.CompilerParams(
            collective_id=0, has_side_effects=True, vmem_limit_bytes=60 * 1024 * 1024
        ),
    )(
        hidden, memory, lengths, memory_lengths, jnp.swapaxes(routes, 1, 2),
        jnp.swapaxes(norm_gain, 0, 1), jnp.swapaxes(router, 1, 2),
        w_in, w_out, shortlist, student, targets,
    )
    return layer_out, loss[0, 0]


def solution(mesh):
    placed = (
        P("segment", "expert", None),
        P("segment", "expert", None),
        P("segment", "expert"),
        P("segment", "expert"),
        P("segment", "expert", None),
        P("segment", None, None),
        P("segment", None, None),
        P("segment", None, "expert"),
        P("segment", "expert", None),
        P("segment", None, None),
        P("segment", "expert", None),
        P("segment", "expert"),
    )
    return jax.shard_map(
        local,
        mesh=mesh,
        in_specs=placed,
        out_specs=(P("segment", "expert", None), P()),
        check_vma=False,
    )
```

profile of v0, /device:TPU:0, one launch (start us, length us, event | category | flops | bytes accessed | tf_op | source)
XLA Modules:
  0.0 60.8 jit_solution(9523053632223755384)
XLA Ops:
  1.9 55.5 %shard_map.131 = (bf16[1,32,2048]{2,1,0:T(8,128)(2,1)}, f32[1,1]{1,0:T(1,128)}) custom-call(bf16[1,32,2048]{2,1,0:T(8,128)(2,1)} %hidden_any.1, bf16[1,32,2048]{2,1,0:T(8,128)(2,1)} %memory.1, s32[1,1]{1,0:T(1,128)S(6)} %copy.16.lengths, s32[1,1]{1,0:T(1,128)S(6)} %copy.17.memory_lengths, s32[1,2,32]{2,1,0:T(2,128)} %bitcast.6, f32[3,1,2048]{2,1,0:T(1,128)} %bitcast.4, ...), custom_call_target="tpu_custom_call" | custom-call | tf_op jit(solution)/shard_map/pallas_call | solution.py:498
  57.4 1.6 %copy.18 = bf16[1,32,2048]{2,1,0:T(8,128)(2,1)} copy(bf16[1,32,2048]{2,1,0:T(8,128)(2,1)} %get-tuple-element.8) | data formatting | bytes 262144
where the time goes:
time: 61 us; the launch traced here: 60.8 us
  Pallas kernels  55.5 us (91%)
  between operations  3.74 us (6%)
  local copies, waits for them, and re-layouts  1.57 us (3%)
    pallas_call x1, Pallas kernels, local(): pl.pallas_call(functools.partial(kernel, n_seg, n_exp, experts, gx, gc),...  55.5 us
    unnamed x1, local copies, waits for them, and re-layouts  1.57 us

commit v1 on v0

v1 whole, which is shorter than its diff:
```python
import functools
import math

import jax
import jax.numpy as jnp
from jax import lax
from jax.experimental import pallas as pl
from jax.experimental.pallas import tpu as pltpu
from jax.sharding import PartitionSpec as P

HEAD_DIM = 128
LEN = 32
EPS = 1e-05
MESH = pl.DeviceIdType.MESH
BF = jnp.bfloat16
F32 = jnp.float32


def layer_norm(values, gain_row):
    centred = values - jnp.mean(values, axis=-1, keepdims=True)
    spread = jnp.mean(centred * centred, axis=-1, keepdims=True)
    return centred * lax.rsqrt(spread + EPS) * gain_row


def xor(a, k, count):
    out = 0
    bit = 1
    while bit < count:
        out = out + lax.rem(a // bit + (k // bit) % 2, 2) * bit
        bit *= 2
    return out


def kernel(
    n_seg, n_exp, experts, gx, gc,
    hidden_any, memory, lengths, memory_lengths, routes_any, gain_any, router_any,
    w_in, w_out, shortlist, student_any, targets,
    layer_out, loss_out,
    hidden, routes, norm_gain, router, student, out_stage,
    win, wout, short, kmem, klen_src, klen, mid,
    out_a, out_b, x, x_b, stage, act, y0,
    core, rc, xs_a, xs_b, rx_a, rx_b, zs_a, zs_b, z_a, z_b, z_all, z_stage,
    lsend, lrecv, lwide, tally,
    wsem, msem, ra, rb, rc_r, rx_r, rz_r, sent, l_s, l_r,
):
    seg = lax.axis_index("segment")
    me = lax.axis_index("expert")
    half_seg = n_seg // 2
    group = gx * gc
    e = me // group
    j = lax.rem(me, group)
    xi = j // gc
    ci = lax.rem(j, gc)
    tok = hidden.shape[1]
    width = hidden.shape[2]
    heads = width // HEAD_DIM
    cap = 5 * tok // 8
    main = cap // 16 * 16
    rest = cap - main
    hop_order = list(range(1, experts))

    def peer(ds, d):
        return (lax.rem(seg + ds, n_seg), lax.rem(me + d, n_exp))

    def dev(e2, x2, c2):
        return (seg, (e2 * gx + x2) * gc + c2)

    barrier = pltpu.get_barrier_semaphore()
    for ds in range(n_seg):
        for d in range(n_exp):
            if ds or d:
                pl.semaphore_signal(
                    barrier, inc=1, device_id=peer(ds, d), device_id_type=MESH
                )

    early = [
        pltpu.make_async_copy(hidden_any, hidden, wsem.at[3]),
        pltpu.make_async_copy(gain_any, norm_gain, wsem.at[4]),
        pltpu.make_async_copy(routes_any, routes, wsem.at[5]),
        pltpu.make_async_copy(router_any, router, wsem.at[6]),
        pltpu.make_async_copy(student_any, student, wsem.at[7]),
    ]
    for load in early:
        load.start()
    loads = [
        pltpu.make_async_copy(w_in.at[0], win, wsem.at[0]),
        pltpu.make_async_copy(w_out.at[0], wout, wsem.at[1]),
        pltpu.make_async_copy(shortlist.at[0], short, wsem.at[2]),
    ]
    for load in loads:
        load.start()

    klen_src[...] = jnp.broadcast_to(memory_lengths[0:1, 0:1], klen_src.shape)
    for q in range(1, tok // LEN):
        klen_src[q : q + 1, :] = jnp.broadcast_to(memory_lengths[0:1, q : q + 1], (1, 128))
    pl.semaphore_wait(barrier, n_exp * n_seg - 1)

    is_decoder = seg >= half_seg
    to_seg = lax.rem(seg + half_seg, n_seg)
    groups = 4
    band = width // groups
    mem_copies = [
        pltpu.make_async_remote_copy(
            memory.at[0, :, g * band : (g + 1) * band], kmem.at[:, g * band : (g + 1) * band],
            msem.at[2], msem.at[3 + g], device_id=(to_seg, me), device_id_type=MESH,
        )
        for g in range(groups)
    ]
    len_copy = pltpu.make_async_remote_copy(
        klen_src, klen, msem.at[0], msem.at[1], device_id=(to_seg, me), device_id_type=MESH
    )

    @pl.when(seg < half_seg)
    def _():
        len_copy.start()
        for copy in mem_copies:
            copy.start()

    early[0].wait()
    early[1].wait()
    gains = [norm_gain[i] for i in range(3)]
    states = hidden[0].astype(F32)

    @pl.when(seg < half_seg)
    def _():
        mid[...] = states

    @pl.when(seg >= half_seg)
    def _():
        queries = layer_norm(states, gains[0]).astype(BF)
        len_copy.wait_recv()
        col = lax.broadcasted_iota(jnp.int32, (tok, tok), 1)
        row = lax.broadcasted_iota(jnp.int32, (tok, tok), 0)
        klen_v = klen[...]
        allowed = jnp.zeros((tok, tok), jnp.bool_)
        for q in range(tok // LEN):
            inside = (col >= q * LEN) & (col - q * LEN < klen_v[q : q + 1, 0:1])
            inside = inside & (col < (q + 1) * LEN) & (row >= q * LEN) & (row < (q + 1) * LEN)
            allowed = allowed | inside
        for g in range(groups):
            mem_copies[g].wait_recv()
            keys = kmem[:, g * band : (g + 1) * band]
            parts = [slice(h * HEAD_DIM, (h + 1) * HEAD_DIM) for h in range(band // HEAD_DIM)]
            scores = jnp.concatenate(
                [
                    jnp.where(
                        allowed,
                        lax.dot_general(
                            queries[:, g * band + part.start : g * band + part.stop], keys[:, part],
                            (((1,), (1,)), ((), ())), preferred_element_type=F32,
                        )
                        * (1.0 / math.sqrt(HEAD_DIM)),
                        -1e30,
                    )
                    for part in parts
                ],
                axis=0,
            )
            top = jnp.max(scores, axis=-1, keepdims=True)
            raised = jnp.exp(scores - top)
            weights = (raised / jnp.sum(raised, axis=-1, keepdims=True)).astype(BF)
            for h, part in enumerate(parts):
                here = slice(g * band + part.start, g * band + part.stop)
                mid[:, here] = states[:, here] + jnp.dot(
                    weights[h * tok : (h + 1) * tok], keys[:, part], preferred_element_type=F32
                )

    normed = layer_norm(mid[...], gains[1]).astype(BF)

    early[2].wait()
    expert_lane = lax.broadcasted_iota(jnp.int32, (tok, experts), 1)
    pos = lax.broadcasted_iota(jnp.int32, (tok, 1), 0)
    valid = jnp.zeros((tok, 1), F32)
    for q in range(tok // LEN):
        ok = (pos >= q * LEN) & (pos < (q + 1) * LEN) & (pos - q * LEN < lengths[0:1, q : q + 1])
        valid = valid + ok.astype(F32)
    square = lax.broadcasted_iota(jnp.int32, (tok, tok), 0) == lax.broadcasted_iota(
        jnp.int32, (tok, tok), 1
    )

    def column(row):
        spread = jnp.where(square, jnp.broadcast_to(row, (tok, tok)), 0)
        return jnp.sum(spread.astype(F32), axis=-1, keepdims=True)

    expert_lane = expert_lane.astype(F32)
    first_hot = (column(routes[0, 0:1, :]) == expert_lane).astype(F32)
    second_hot = (column(routes[0, 1:2, :]) == expert_lane).astype(F32)
    chosen = (first_hot + second_hot) * valid
    before = (
        lax.broadcasted_iota(jnp.int32, (tok, tok), 1)
        < lax.broadcasted_iota(jnp.int32, (tok, tok), 0)
    ).astype(BF)
    rank = jnp.dot(before, chosen.astype(BF), preferred_element_type=F32)
    n_main = experts * main
    n_slots = experts * cap
    lanes = -(-n_slots // 128) * 128
    lane = lax.broadcasted_iota(jnp.int32, (1, lanes), 1)
    slot_of = jnp.full((1, lanes), -1, jnp.int32)
    expert_of = jnp.full((1, lanes), -1, jnp.int32)
    for k in range(experts):
        ek = xor(e, k, experts)
        in_main = (lane >= k * main) & (lane < (k + 1) * main)
        low = n_main + k * rest
        in_rest = (lane >= low) & (lane < low + rest)
        slot_of = jnp.where(in_main, lane - k * main, slot_of)
        slot_of = jnp.where(in_rest, lane - low + main, slot_of)
        expert_of = jnp.where(in_main | in_rest, ek, expert_of)
    placing = jnp.zeros((tok, lanes), F32)
    for k in range(experts):
        here = (expert_of == k) & (rank[:, k : k + 1] == slot_of.astype(F32))
        placing = placing + jnp.where(here, chosen[:, k : k + 1], 0.0)
    place_rows = jnp.transpose(placing)[0:n_slots].astype(BF)
    slots = jnp.dot(place_rows, normed, preferred_element_type=F32)

    chunk = gc * gx * cap
    side = gx * cap
    side_main = gx * main
    half_width = width // 2
    halves = [slice(h * half_width, (h + 1) * half_width) for h in range(2)]

    def rows_a(dc, dx, k):
        return pl.ds(k * chunk + dc * side + dx * main, main)

    def index_b(dc, dx, k):
        return (dc * gx + dx) * experts + k

    for k in hop_order:
        out_a[k] = slots[k * main : (k + 1) * main].astype(BF)
        out_b[k] = slots[n_main + k * rest : n_main + (k + 1) * rest].astype(BF)
    x[rows_a(0, 0, 0), :] = slots[0:main].astype(BF)
    x_b[0] = slots[n_main : n_main + rest].astype(BF)

    def send(src, dst, r_sem, target):
        pltpu.make_async_remote_copy(
            src, dst, sent, r_sem, device_id=target, device_id_type=MESH
        ).start()

    def landed(ref, sem):
        pltpu.make_async_copy(ref, ref, sem).wait()

    def count(size, sem):
        landed(tally.at[0 : size // 1024], sem)

    def piece(slot, p):
        if p < 2:
            return x.at[rows_a(*slot), halves[p]]
        return x_b.at[index_b(*slot)]

    def mark(slot, p):
        if slot[0]:
            return rb.at[slot[1] * experts + slot[2]]
        return ra.at[2 * (slot[1] * experts + slot[2]) + min(p, 1)]

    def arrived(slot, p):
        if p == 0:
            landed(piece(slot, 0), mark(slot, 0))
        elif p == 1:
            count(main * half_width + rest * width, mark(slot, 1))

    def forward(slot_from, slot_to, p, target):
        send(piece(slot_from, p), piece(slot_to, p), mark(slot_to, p), target)

    for k in hop_order:
        target = dev(xor(e, k, experts), xi, ci)
        for p in range(3):
            src = out_a.at[k, :, halves[p]] if p < 2 else out_b.at[k]
            send(src, piece((0, 0, k), p), mark((0, 0, k), p), target)

    core_dev = dev(e, xi, lax.rem(ci + 1, gc))

    def from_column(k):
        for p in range(3):
            if k:
                arrived((0, 0, k), p)
            for d in range(1, gx):
                forward((0, 0, k), (0, d, k), p, dev(e, lax.rem(xi + d, gx), ci))
            forward((0, 0, k), (1, 0, k), p, core_dev)

    def from_chips(k):
        for p in range(3):
            for d in range(1, gx):
                arrived((0, d, k), p)
                forward((0, d, k), (1, d, k), p, core_dev)

    units = win.shape[1]
    tile = min(512, units)
    tile2 = min(512, half_width)

    def first(k):
        for d in range(gx):
            count(cap * width, mark((1, d, k), 0))
        for dc in range(gc):
            for d in range(gx):
                stage[d * rest : (d + 1) * rest, :] = x_b[index_b(dc, d, k)].astype(F32)
            low = k * chunk + dc * side + side_main
            x[low : low + gx * rest, :] = stage[...].astype(BF)
        if k == 0:
            loads[0].wait()
        rows = slice(k * chunk, (k + 1) * chunk)

        @pl.loop(0, units // tile)
        def _(i):
            cols = pl.ds(pl.multiple_of(i * tile, tile), tile)
            act[:, cols] = jnp.maximum(
                jnp.dot(x[rows, :], win[:, cols], preferred_element_type=F32), 0.0
            ).astype(BF)

    def second(k):
        if k == 0:
            loads[1].wait()
        for h in range(2):
            @pl.loop(0, half_width // tile2)
            def _(i):
                cols = pl.ds(pl.multiple_of(h * half_width + i * tile2, tile2), tile2)
                part = jnp.dot(act[...], wout[:, cols], preferred_element_type=F32)
                core[k, :, cols] = part[side:].astype(BF)
                y0[k, :, cols] = part[0:side]

            send(core.at[k, :, halves[h]], rc.at[k, :, halves[h]], rc_r.at[2 * k + h], core_dev)

    def to_chips(k):
        for h in range(2):
            part = halves[h]
            landed(rc.at[k, :, part], rc_r.at[2 * k + h])
            tail = y0[k, side_main:, part] + rc[k, side_main:, part].astype(F32)
            for d in range(1, gx):
                o = (d - 1) * experts + k
                rows = slice(d * main, (d + 1) * main)
                xs_a[o, :, part] = (y0[k, rows, part] + rc[k, rows, part].astype(F32)).astype(BF)
                xs_b[o, :, part] = tail[d * rest : (d + 1) * rest].astype(BF)
                target = dev(e, lax.rem(xi + gx - d, gx), ci)
                for src, dst in [(xs_a, rx_a), (xs_b, rx_b)]:
                    send(src.at[o, :, part], dst.at[o, :, part], rx_r.at[2 * o + h], target)

    def to_column(k):
        for h in range(2):
            part = halves[h]
            sum_a = y0[k, 0:main, part] + rc[k, 0:main, part].astype(F32)
            tail = y0[k, side_main:, part] + rc[k, side_main:, part].astype(F32)
            sum_b = tail[0:rest]
            for d in range(1, gx):
                o = (d - 1) * experts + k
                count(cap * half_width, rx_r.at[2 * o + h])
                sum_a = sum_a + rx_a[o, :, part].astype(F32)
                sum_b = sum_b + rx_b[o, :, part].astype(F32)
            if k:
                zs_a[k, :, part] = sum_a.astype(BF)
                zs_b[k, :, part] = sum_b.astype(BF)
                target = dev(xor(e, k, experts), xi, ci)
                for src, dst in [(zs_a, z_a), (zs_b, z_b)]:
                    send(src.at[k, :, part], dst.at[k, :, part], rz_r.at[2 * k + h], target)
            else:
                z_all[0:main, part] = sum_a.astype(BF)
                z_stage[0:rest, part] = sum_b

    last = experts - 1
    from_column(0)
    from_chips(0)
    if last:
        from_column(1)
    for k in range(experts):
        first(k)
        if k:
            to_chips(k - 1)
            if k + 1 <= last:
                from_chips(k + 1)
        second(k)
        if k == 0:
            if last:
                from_chips(1)
            for relay in range(2, experts):
                from_column(relay)
    to_chips(last)
    for k in range(experts):
        to_column(k)

    early[3].wait()
    probs = lax.dot_general(
        normed, router[0], (((1,), (1,)), ((), ())), preferred_element_type=F32
    )
    probs = jnp.exp(probs - jnp.max(probs, axis=-1, keepdims=True))
    probs = probs / jnp.sum(probs, axis=-1, keepdims=True)
    prob_first = jnp.sum(probs * first_hot, axis=-1, keepdims=True)
    prob_second = jnp.sum(probs * second_hot, axis=-1, keepdims=True)
    gate = (prob_first * first_hot + prob_second * second_hot) / (prob_first + prob_second)
    combine = jnp.zeros((tok, lanes), F32)
    for k in range(experts):
        combine = combine + jnp.where(expert_of == k, gate[:, k : k + 1], 0.0)
    combine = (combine * placing)[:, 0:n_slots]
    high = combine.astype(BF)
    low = (combine - high.astype(F32)).astype(BF)

    early[4].wait()
    learner_in = student[0]
    shifted = learner_in - jnp.max(learner_in, axis=-1, keepdims=True)
    learner = shifted - jnp.log(jnp.sum(jnp.exp(shifted), axis=-1, keepdims=True))
    target_col = column(targets[0:1, :])
    vocab = student.shape[2]
    picked = lax.broadcasted_iota(jnp.int32, (tok, vocab), 1).astype(F32) == target_col
    hit = jnp.sum(jnp.where(picked, learner, 0.0), axis=-1, keepdims=True)
    loads[2].wait()

    for h in range(2):
        part = halves[h]
        for k in hop_order:
            count(cap * half_width, rz_r.at[2 * k + h])
            z_all[k * main : (k + 1) * main, part] = z_a[k, :, part]
            z_stage[k * rest : (k + 1) * rest, part] = z_b[k, :, part].astype(F32)
        z_all[n_main:, part] = z_stage[:, part].astype(BF)
        back = z_all[:, part]
        moe = jnp.dot(high, back, preferred_element_type=F32) + jnp.dot(
            low, back, preferred_element_type=F32
        )
        out_stage[:, part] = (mid[:, part] + moe).astype(BF)
    out = out_stage[...]
    out_copy = pltpu.make_async_copy(out_stage, layer_out.at[0], wsem.at[8])
    out_copy.start()

    final = layer_norm(out.astype(F32), gains[2]).astype(BF)
    logits = jnp.dot(final, short[...], preferred_element_type=F32)
    logits = logits - jnp.max(logits, axis=-1, keepdims=True)
    teacher = logits - jnp.log(jnp.sum(jnp.exp(logits), axis=-1, keepdims=True))
    token_loss = jnp.sum(jnp.exp(teacher) * (teacher - learner), axis=-1, keepdims=True) - hit
    counted = jnp.where(is_decoder, valid, 0.0)
    loss_sum = jnp.sum(token_loss * counted, axis=0, keepdims=True)
    loss_count = jnp.sum(counted, axis=0, keepdims=True)
    spot = lax.broadcasted_iota(jnp.int32, lsend.shape, 1)
    pair = jnp.where(spot == 0, loss_sum, jnp.where(spot == 1, loss_count, 0.0))
    lsend[...] = pair

    mine = (seg - half_seg) * n_exp + me
    n_loss = (n_seg - half_seg) * n_exp

    @pl.when(is_decoder)
    def _():
        lrecv[mine] = pair
        for ds in range(n_seg):
            for d in range(n_exp):
                if ds or d:
                    pltpu.make_async_remote_copy(
                        lsend, lrecv.at[mine], l_s, l_r,
                        device_id=peer(ds, d), device_id_type=MESH,
                    ).start()
        landed(lrecv.at[0 : n_loss - 1], l_r)

    @pl.when(seg < half_seg)
    def _():
        landed(lrecv, l_r)

    total = lrecv[0]
    for i in range(1, (n_seg - half_seg) * n_exp):
        total = total + lrecv[i]
    loss_out[...] = total[0:1, 0:1] / total[0:1, 1:2]

    @pl.when(is_decoder)
    def _():
        landed(lwide.at[0 : n_seg * n_exp - 1], l_s)

    out_copy.wait()
    moved = 2 * cap * (experts - 1 + (2 * gx - 1) * experts)
    left = moved * width // units
    while left:
        step = min(left, win.shape[0])
        landed(win.at[0:step], sent)
        left -= step

    @pl.when(seg < half_seg)
    def _():
        landed(kmem, msem.at[2])
        len_copy.wait_send()


def local(
    hidden, memory, lengths, memory_lengths, routes, norm_gain, router,
    w_in, w_out, shortlist, student, targets,
):
    n_seg = lax.axis_size("segment")
    n_exp = lax.axis_size("expert")
    experts = router.shape[2]
    group = n_exp // experts
    gc = 2
    gx = group // gc
    tok, width = hidden.shape[1], hidden.shape[2]
    units = w_in.shape[2]
    vocab = shortlist.shape[2]
    cap = 5 * tok // 8
    main = cap // 16 * 16
    rest = cap - main
    blocks = gx * experts
    vm = pl.BlockSpec(memory_space=pltpu.VMEM)
    hbm = pl.BlockSpec(memory_space=pl.ANY)
    v = pltpu.VMEM
    dma = pltpu.SemaphoreType.DMA
    nx = max(gx - 1, 1) * experts
    scratch = [
        v((1, tok, width), BF), v((1, 2, tok), jnp.int32), v((3, 1, width), F32),
        v((1, experts, width), BF), v((1, tok, vocab), F32), v((tok, width), BF),
        v((width, units), BF), v((units, width), BF), v((width, vocab), BF),
        v((tok, width), BF), v((8, 128), jnp.int32), v((8, 128), jnp.int32), v((tok, width), F32),
        v((experts, main, width), BF), v((experts, rest, width), BF),
        v((experts * gc * gx * cap, width), BF), v((gc * blocks, rest, width), BF),
        v((gx * rest, width), F32), v((gc * gx * cap, units), BF),
        v((experts, gx * cap, width), F32),
        v((experts, gx * cap, width), BF), v((experts, gx * cap, width), BF),
        v((nx, main, width), BF), v((nx, rest, width), BF),
        v((nx, main, width), BF), v((nx, rest, width), BF),
        v((experts, main, width), BF), v((experts, rest, width), BF),
        v((experts, main, width), BF), v((experts, rest, width), BF),
        v((experts * cap, width), BF), v((experts * rest, width), F32),
        v((1, 128), F32), v(((n_seg - n_seg // 2) * n_exp, 1, 128), F32),
        v((n_seg * n_exp, 1, 128), F32), v((cap * width // 1024, 8, 128), BF),
        dma((9,)), dma((7,)), dma((2 * blocks,)), dma((blocks,)),
        dma((2 * experts,)), dma((2 * nx,)), dma((2 * experts,)),
        dma(()), dma(()), dma(()),
    ]
    layer_out, loss = pl.pallas_call(
        functools.partial(kernel, n_seg, n_exp, experts, gx, gc),
        out_shape=(
            jax.ShapeDtypeStruct((1, tok, width), BF),
            jax.ShapeDtypeStruct((1, 1), F32),
        ),
        in_specs=[hbm, hbm, vm, vm, hbm, hbm, hbm, hbm, hbm, hbm, hbm, vm],
        out_specs=(hbm, vm),
        scratch_shapes=scratch,
        compiler_params=pltpu.CompilerParams(
            collective_id=0, has_side_effects=True, vmem_limit_bytes=60 * 1024 * 1024
        ),
    )(
        hidden, memory, lengths, memory_lengths, jnp.swapaxes(routes, 1, 2),
        jnp.swapaxes(norm_gain, 0, 1), jnp.swapaxes(router, 1, 2),
        w_in, w_out, shortlist, student, targets,
    )
    return layer_out, loss[0, 0]


def solution(mesh):
    placed = (
        P("segment", "expert", None),
        P("segment", "expert", None),
        P("segment", "expert"),
        P("segment", "expert"),
        P("segment", "expert", None),
        P("segment", None, None),
        P("segment", None, None),
        P("segment", None, "expert"),
        P("segment", "expert", None),
        P("segment", None, None),
        P("segment", "expert", None),
        P("segment", "expert"),
    )
    return jax.shard_map(
        local,
        mesh=mesh,
        in_specs=placed,
        out_specs=(P("segment", "expert", None), P()),
        check_vma=False,
    )
```

time: 61 us -> 53.7 us (0.88)
  Pallas kernels: 55.5 us -> 48.2 us
    pallas_call x1, Pallas kernels: 55.5 us -> 48.2 us  [local(): pl.pallas_call(functools.partial(kernel, n_seg, n_exp, experts, gx, gc),...]
where the time goes in v1:
time: 53.7 us; the launch traced here: 53.5 us
  Pallas kernels  48.2 us (90%)
  between operations  3.74 us (7%)
  local copies, waits for them, and re-layouts  1.57 us (3%)
    pallas_call x1, Pallas kernels, local(): pl.pallas_call(functools.partial(kernel, n_seg, n_exp, experts, gx, gc),...  48.2 us
    unnamed x1, local copies, waits for them, and re-layouts  1.57 us

profile of v1, /device:TPU:0, one launch (start us, length us, event | category | flops | bytes accessed | tf_op | source)
XLA Modules:
  0.0 53.5 jit_solution(2086353613601914374)
XLA Ops:
  1.9 48.2 %shard_map.131 = (bf16[1,32,2048]{2,1,0:T(8,128)(2,1)}, f32[1,1]{1,0:T(1,128)}) custom-call(bf16[1,32,2048]{2,1,0:T(8,128)(2,1)} %hidden_any.1, bf16[1,32,2048]{2,1,0:T(8,128)(2,1)} %memory.1, s32[1,1]{1,0:T(1,128)S(6)} %copy.16.lengths, s32[1,1]{1,0:T(1,128)S(6)} %copy.17.memory_lengths, s32[1,2,32]{2,1,0:T(2,128)} %bitcast.6, f32[3,1,2048]{2,1,0:T(1,128)} %bitcast.4, ...), custom_call_target="tpu_custom_call" | custom-call | tf_op jit(solution)/shard_map/pallas_call | solution.py:516
  50.1 1.6 %copy.18 = bf16[1,32,2048]{2,1,0:T(8,128)(2,1)} copy(bf16[1,32,2048]{2,1,0:T(8,128)(2,1)} %get-tuple-element.8) | data formatting | bytes 262144

commit v2 on v1

--- a/solution.py
+++ b/solution.py
@@ -41,7 +41,7 @@
     out_a, out_b, x, x_b, stage, act, y0,
     core, rc, xs_a, xs_b, rx_a, rx_b, zs_a, zs_b, z_a, z_b, z_all, z_stage,
     lsend, lrecv, lwide, tally,
-    wsem, msem, ra, rb, rc_r, rx_r, rz_r, sent, l_s, l_r,
+    wsem, msem, ra, rb, rc_r, rx_r, rz_r, sent, l_s, l_r, met,
 ):
     seg = lax.axis_index("segment")
     me = lax.axis_index("expert")
@@ -66,12 +66,22 @@
         return (seg, (e2 * gx + x2) * gc + c2)
 
     barrier = pltpu.get_barrier_semaphore()
-    for ds in range(n_seg):
-        for d in range(n_exp):
-            if ds or d:
-                pl.semaphore_signal(
-                    barrier, inc=1, device_id=peer(ds, d), device_id_type=MESH
-                )
+    to_seg = lax.rem(seg + half_seg, n_seg)
+    sides = [((e > 0), (lax.rem(e + experts - 1, experts))), ((e < experts - 1), lax.rem(e + 1, experts))]
+    beside = (e > 0).astype(jnp.int32) + (e < experts - 1).astype(jnp.int32)
+
+    def greet(sem):
+        for there, e2 in sides:
+            @pl.when(there)
+            def _():
+                pl.semaphore_signal(sem, inc=1, device_id=dev(e2, xi, ci), device_id_type=MESH)
+
+    near = [(to_seg, me)]
+    near += [dev(e, lax.rem(xi + d, gx), ci) for d in range(1, gx)]
+    near += [dev(e, xi, lax.rem(ci + d, gc)) for d in range(1, gc)]
+    for device in near:
+        pl.semaphore_signal(barrier, inc=1, device_id=device, device_id_type=MESH)
+    greet(barrier)
 
     early = [
         pltpu.make_async_copy(hidden_any, hidden, wsem.at[3]),
@@ -93,10 +103,9 @@
     klen_src[...] = jnp.broadcast_to(memory_lengths[0:1, 0:1], klen_src.shape)
     for q in range(1, tok // LEN):
         klen_src[q : q + 1, :] = jnp.broadcast_to(memory_lengths[0:1, q : q + 1], (1, 128))
-    pl.semaphore_wait(barrier, n_exp * n_seg - 1)
+    pl.semaphore_wait(barrier, len(near) + beside)
 
     is_decoder = seg >= half_seg
-    to_seg = lax.rem(seg + half_seg, n_seg)
     groups = 4
     band = width // groups
     mem_copies = [
@@ -116,6 +125,9 @@
         for copy in mem_copies:
             copy.start()
 
+    rounds = max(experts - 2, 0)
+    if rounds:
+        greet(met.at[0])
     early[0].wait()
     early[1].wait()
     gains = [norm_gain[i] for i in range(3)]
@@ -165,6 +177,11 @@
                     weights[h * tok : (h + 1) * tok], keys[:, part], preferred_element_type=F32
                 )
 
+    for i in range(rounds):
+        pl.semaphore_wait(met.at[i], beside)
+        if i + 1 < rounds:
+            greet(met.at[i + 1])
+
     normed = layer_norm(mid[...], gains[1]).astype(BF)
 
     early[2].wait()
@@ -283,8 +300,8 @@
                 forward((0, d, k), (1, d, k), p, core_dev)
 
     units = win.shape[1]
-    tile = min(512, units)
-    tile2 = min(512, half_width)
+    tile = min(1024, units)
+    tile2 = min(1024, half_width)
 
     def first(k):
         for d in range(gx):
@@ -362,9 +379,11 @@
         first(k)
         if k:
             to_chips(k - 1)
-            if k + 1 <= last:
-                from_chips(k + 1)
+        if k > 1 and k + 1 <= last:
+            from_chips(k + 1)
         second(k)
+        if k == 1 and k + 1 <= last:
+            from_chips(k + 1)
         if k == 0:
             if last:
                 from_chips(1)
@@ -511,7 +530,7 @@
         v((n_seg * n_exp, 1, 128), F32), v((cap * width // 1024, 8, 128), BF),
         dma((9,)), dma((7,)), dma((2 * blocks,)), dma((blocks,)),
         dma((2 * experts,)), dma((2 * nx,)), dma((2 * experts,)),
-        dma(()), dma(()), dma(()),
+        dma(()), dma(()), dma(()), pltpu.SemaphoreType.REGULAR((max(experts - 2, 1),)),
     ]
     layer_out, loss = pl.pallas_call(
         functools.partial(kernel, n_seg, n_exp, experts, gx, gc),

time: 53.7 us -> 51.3 us (0.955)
  Pallas kernels: 48.2 us -> 45.8 us
    pallas_call x1, Pallas kernels: 48.2 us -> 45.8 us  [local(): pl.pallas_call(functools.partial(kernel, n_seg, n_exp, experts, gx, gc),...]
where the time goes in v2:
time: 51.3 us; the launch traced here: 51.1 us
  Pallas kernels  45.8 us (89%)
  between operations  3.74 us (7%)
  local copies, waits for them, and re-layouts  1.57 us (3%)
    pallas_call x1, Pallas kernels, local(): pl.pallas_call(functools.partial(kernel, n_seg, n_exp, experts, gx, gc),...  45.8 us
    unnamed x1, local copies, waits for them, and re-layouts  1.57 us

profile of v2, /device:TPU:0, one launch (start us, length us, event | category | flops | bytes accessed | tf_op | source)
XLA Modules:
  0.0 51.1 jit_solution(840928297182010535)
XLA Ops:
  1.9 45.8 %shard_map.131 = (bf16[1,32,2048]{2,1,0:T(8,128)(2,1)}, f32[1,1]{1,0:T(1,128)}) custom-call(bf16[1,32,2048]{2,1,0:T(8,128)(2,1)} %hidden_any.1, bf16[1,32,2048]{2,1,0:T(8,128)(2,1)} %memory.1, s32[1,1]{1,0:T(1,128)S(6)} %copy.16.lengths, s32[1,1]{1,0:T(1,128)S(6)} %copy.17.memory_lengths, s32[1,2,32]{2,1,0:T(2,128)} %bitcast.6, f32[3,1,2048]{2,1,0:T(1,128)} %bitcast.4, ...), custom_call_target="tpu_custom_call" | custom-call | tf_op jit(solution)/shard_map/pallas_call | solution.py:535
  47.8 1.6 %copy.18 = bf16[1,32,2048]{2,1,0:T(8,128)(2,1)} copy(bf16[1,32,2048]{2,1,0:T(8,128)(2,1)} %get-tuple-element.8) | data formatting | bytes 262144

commit v3 on v2

--- a/solution.py
+++ b/solution.py
@@ -97,9 +97,6 @@
         pltpu.make_async_copy(w_out.at[0], wout, wsem.at[1]),
         pltpu.make_async_copy(shortlist.at[0], short, wsem.at[2]),
     ]
-    for load in loads:
-        load.start()
-
     klen_src[...] = jnp.broadcast_to(memory_lengths[0:1, 0:1], klen_src.shape)
     for q in range(1, tok // LEN):
         klen_src[q : q + 1, :] = jnp.broadcast_to(memory_lengths[0:1, q : q + 1], (1, 128))
@@ -125,6 +122,9 @@
         for copy in mem_copies:
             copy.start()
 
+    for load in loads:
+        load.start()
+
     rounds = max(experts - 2, 0)
     if rounds:
         greet(met.at[0])
@@ -133,13 +133,60 @@
     gains = [norm_gain[i] for i in range(3)]
     states = hidden[0].astype(F32)
 
+    queries = layer_norm(states, gains[0]).astype(BF)
+    for i in range(rounds - 1):
+        pl.semaphore_wait(met.at[i], beside)
+        greet(met.at[i + 1])
+
+    early[2].wait()
+    expert_lane = lax.broadcasted_iota(jnp.int32, (tok, experts), 1)
+    pos = lax.broadcasted_iota(jnp.int32, (tok, 1), 0)
+    valid = jnp.zeros((tok, 1), F32)
+    for q in range(tok // LEN):
+        ok = (pos >= q * LEN) & (pos < (q + 1) * LEN) & (pos - q * LEN < lengths[0:1, q : q + 1])
+        valid = valid + ok.astype(F32)
+    square = lax.broadcasted_iota(jnp.int32, (tok, tok), 0) == lax.broadcasted_iota(
+        jnp.int32, (tok, tok), 1
+    )
+
+    def column(row):
+        spread = jnp.where(square, jnp.broadcast_to(row, (tok, tok)), 0)
+        return jnp.sum(spread.astype(F32), axis=-1, keepdims=True)
+
+    expert_lane = expert_lane.astype(F32)
+    first_hot = (column(routes[0, 0:1, :]) == expert_lane).astype(F32)
+    second_hot = (column(routes[0, 1:2, :]) == expert_lane).astype(F32)
+    chosen = (first_hot + second_hot) * valid
+    before = (
+        lax.broadcasted_iota(jnp.int32, (tok, tok), 1)
+        < lax.broadcasted_iota(jnp.int32, (tok, tok), 0)
+    ).astype(BF)
+    rank = jnp.dot(before, chosen.astype(BF), preferred_element_type=F32)
+    n_main = experts * main
+    n_slots = experts * cap
+    lanes = -(-n_slots // 128) * 128
+    lane = lax.broadcasted_iota(jnp.int32, (1, lanes), 1)
+    slot_of = jnp.full((1, lanes), -1, jnp.int32)
+    expert_of = jnp.full((1, lanes), -1, jnp.int32)
+    for k in range(experts):
+        ek = xor(e, k, experts)
+        in_main = (lane >= k * main) & (lane < (k + 1) * main)
+        low = n_main + k * rest
+        in_rest = (lane >= low) & (lane < low + rest)
+        slot_of = jnp.where(in_main, lane - k * main, slot_of)
+        slot_of = jnp.where(in_rest, lane - low + main, slot_of)
+        expert_of = jnp.where(in_main | in_rest, ek, expert_of)
+    placing = jnp.zeros((tok, lanes), F32)
+    for k in range(experts):
+        here = (expert_of == k) & (rank[:, k : k + 1] == slot_of.astype(F32))
+        placing = placing + jnp.where(here, chosen[:, k : k + 1], 0.0)
+    place_rows = jnp.transpose(placing)[0:n_slots].astype(BF)
     @pl.when(seg < half_seg)
     def _():
         mid[...] = states
 
     @pl.when(seg >= half_seg)
     def _():
-        queries = layer_norm(states, gains[0]).astype(BF)
         len_copy.wait_recv()
         col = lax.broadcasted_iota(jnp.int32, (tok, tok), 1)
         row = lax.broadcasted_iota(jnp.int32, (tok, tok), 0)
@@ -177,56 +224,11 @@
                     weights[h * tok : (h + 1) * tok], keys[:, part], preferred_element_type=F32
                 )
 
-    for i in range(rounds):
-        pl.semaphore_wait(met.at[i], beside)
-        if i + 1 < rounds:
-            greet(met.at[i + 1])
+    if rounds:
+        pl.semaphore_wait(met.at[rounds - 1], beside)
 
     normed = layer_norm(mid[...], gains[1]).astype(BF)
 
-    early[2].wait()
-    expert_lane = lax.broadcasted_iota(jnp.int32, (tok, experts), 1)
-    pos = lax.broadcasted_iota(jnp.int32, (tok, 1), 0)
-    valid = jnp.zeros((tok, 1), F32)
-    for q in range(tok // LEN):
-        ok = (pos >= q * LEN) & (pos < (q + 1) * LEN) & (pos - q * LEN < lengths[0:1, q : q + 1])
-        valid = valid + ok.astype(F32)
-    square = lax.broadcasted_iota(jnp.int32, (tok, tok), 0) == lax.broadcasted_iota(
-        jnp.int32, (tok, tok), 1
-    )
-
-    def column(row):
-        spread = jnp.where(square, jnp.broadcast_to(row, (tok, tok)), 0)
-        return jnp.sum(spread.astype(F32), axis=-1, keepdims=True)
-
-    expert_lane = expert_lane.astype(F32)
-    first_hot = (column(routes[0, 0:1, :]) == expert_lane).astype(F32)
-    second_hot = (column(routes[0, 1:2, :]) == expert_lane).astype(F32)
-    chosen = (first_hot + second_hot) * valid
-    before = (
-        lax.broadcasted_iota(jnp.int32, (tok, tok), 1)
-        < lax.broadcasted_iota(jnp.int32, (tok, tok), 0)
-    ).astype(BF)
-    rank = jnp.dot(before, chosen.astype(BF), preferred_element_type=F32)
-    n_main = experts * main
-    n_slots = experts * cap
-    lanes = -(-n_slots // 128) * 128
-    lane = lax.broadcasted_iota(jnp.int32, (1, lanes), 1)
-    slot_of = jnp.full((1, lanes), -1, jnp.int32)
-    expert_of = jnp.full((1, lanes), -1, jnp.int32)
-    for k in range(experts):
-        ek = xor(e, k, experts)
-        in_main = (lane >= k * main) & (lane < (k + 1) * main)
-        low = n_main + k * rest
-        in_rest = (lane >= low) & (lane < low + rest)
-        slot_of = jnp.where(in_main, lane - k * main, slot_of)
-        slot_of = jnp.where(in_rest, lane - low + main, slot_of)
-        expert_of = jnp.where(in_main | in_rest, ek, expert_of)
-    placing = jnp.zeros((tok, lanes), F32)
-    for k in range(experts):
-        here = (expert_of == k) & (rank[:, k : k + 1] == slot_of.astype(F32))
-        placing = placing + jnp.where(here, chosen[:, k : k + 1], 0.0)
-    place_rows = jnp.transpose(placing)[0:n_slots].astype(BF)
     slots = jnp.dot(place_rows, normed, preferred_element_type=F32)
 
     chunk = gc * gx * cap
@@ -318,7 +320,7 @@
         @pl.loop(0, units // tile)
         def _(i):
             cols = pl.ds(pl.multiple_of(i * tile, tile), tile)
-            act[:, cols] = jnp.maximum(
+            act[k, :, cols] = jnp.maximum(
                 jnp.dot(x[rows, :], win[:, cols], preferred_element_type=F32), 0.0
             ).astype(BF)
 
@@ -329,7 +331,7 @@
             @pl.loop(0, half_width // tile2)
             def _(i):
                 cols = pl.ds(pl.multiple_of(h * half_width + i * tile2, tile2), tile2)
-                part = jnp.dot(act[...], wout[:, cols], preferred_element_type=F32)
+                part = jnp.dot(act[k], wout[:, cols], preferred_element_type=F32)
                 core[k, :, cols] = part[side:].astype(BF)
                 y0[k, :, cols] = part[0:side]
 
@@ -371,26 +373,44 @@
                 z_stage[0:rest, part] = sum_b
 
     last = experts - 1
+
+    def relay(core_side, steps):
+        steps = [(step, k) for step, k in steps if k <= last]
+        if steps:
+            @pl.when((ci > 0) if core_side else (ci == 0))
+            def _():
+                for step, k in steps:
+                    step(k)
+
+    far = range(2, experts)
     from_column(0)
     from_chips(0)
     if last:
         from_column(1)
-    for k in range(experts):
+    relay(1, [(from_column, 2)])
+    first(0)
+    relay(1, [(from_chips, 1), (from_column, 3)])
+    second(0)
+    relay(0, [(from_column, k) for k in far] + [(from_chips, 1)])
+    relay(1, [(from_column, k) for k in far if k > 3] + [(from_chips, 2)])
+    if last:
+        first(1)
+    to_chips(0)
+    relay(0, [(from_chips, 2)])
+    for k in far:
+        relay(1, [(from_chips, k + 1)])
         first(k)
-        if k:
+        relay(0, [(from_chips, k + 1)])
+        if k > 2:
             to_chips(k - 1)
-        if k > 1 and k + 1 <= last:
-            from_chips(k + 1)
         second(k)
-        if k == 1 and k + 1 <= last:
-            from_chips(k + 1)
-        if k == 0:
-            if last:
-                from_chips(1)
-            for relay in range(2, experts):
-                from_column(relay)
-    to_chips(last)
-    for k in range(experts):
+    if last:
+        second(1)
+    if last > 1:
+        to_chips(last)
+    if last:
+        to_chips(1)
+    for k in [*far, *range(min(experts, 2))]:
         to_column(k)
 
     early[3].wait()
@@ -518,7 +538,7 @@
         v((tok, width), BF), v((8, 128), jnp.int32), v((8, 128), jnp.int32), v((tok, width), F32),
         v((experts, main, width), BF), v((experts, rest, width), BF),
         v((experts * gc * gx * cap, width), BF), v((gc * blocks, rest, width), BF),
-        v((gx * rest, width), F32), v((gc * gx * cap, units), BF),
+        v((gx * rest, width), F32), v((experts, gc * gx * cap, units), BF),
         v((experts, gx * cap, width), F32),
         v((experts, gx * cap, width), BF), v((experts, gx * cap, width), BF),
         v((nx, main, width), BF), v((nx, rest, width), BF),

time: 51.3 us -> 48.7 us (0.949)
  Pallas kernels: 45.8 us -> 43.2 us
    pallas_call x1, Pallas kernels: 45.8 us -> 43.2 us  [local(): pl.pallas_call(functools.partial(kernel, n_seg, n_exp, experts, gx, gc),...]
where the time goes in v3:
time: 48.7 us; the launch traced here: 48.5 us
  Pallas kernels  43.2 us (89%)
  between operations  3.74 us (8%)
  local copies, waits for them, and re-layouts  1.57 us (3%)
    pallas_call x1, Pallas kernels, local(): pl.pallas_call(functools.partial(kernel, n_seg, n_exp, experts, gx, gc),...  43.2 us
    unnamed x1, local copies, waits for them, and re-layouts  1.57 us

profile of v3, /device:TPU:0, one launch (start us, length us, event | category | flops | bytes accessed | tf_op | source)
XLA Modules:
  0.0 48.5 jit_solution(17677591873846053525)
XLA Ops:
  1.9 43.2 %shard_map.131 = (bf16[1,32,2048]{2,1,0:T(8,128)(2,1)}, f32[1,1]{1,0:T(1,128)}) custom-call(bf16[1,32,2048]{2,1,0:T(8,128)(2,1)} %hidden_any.1, bf16[1,32,2048]{2,1,0:T(8,128)(2,1)} %memory.1, s32[1,1]{1,0:T(1,128)S(6)} %copy.16.lengths, s32[1,1]{1,0:T(1,128)S(6)} %copy.17.memory_lengths, s32[1,2,32]{2,1,0:T(2,128)} %bitcast.6, f32[3,1,2048]{2,1,0:T(1,128)} %bitcast.4, ...), custom_call_target="tpu_custom_call" | custom-call | tf_op jit(solution)/shard_map/pallas_call | solution.py:555
  45.1 1.6 %copy.18 = bf16[1,32,2048]{2,1,0:T(8,128)(2,1)} copy(bf16[1,32,2048]{2,1,0:T(8,128)(2,1)} %get-tuple-element.8) | data formatting | bytes 262144

commit v4 on v3

--- a/solution.py
+++ b/solution.py
@@ -261,34 +261,32 @@
         landed(tally.at[0 : size // 1024], sem)
 
     def piece(slot, p):
-        if p < 2:
-            return x.at[rows_a(*slot), halves[p]]
+        if p == 0:
+            return x.at[rows_a(*slot), :]
         return x_b.at[index_b(*slot)]
 
     def mark(slot, p):
         if slot[0]:
             return rb.at[slot[1] * experts + slot[2]]
-        return ra.at[2 * (slot[1] * experts + slot[2]) + min(p, 1)]
+        return ra.at[slot[1] * experts + slot[2]]
 
     def arrived(slot, p):
         if p == 0:
-            landed(piece(slot, 0), mark(slot, 0))
-        elif p == 1:
-            count(main * half_width + rest * width, mark(slot, 1))
+            count(cap * width, mark(slot, 0))
 
     def forward(slot_from, slot_to, p, target):
         send(piece(slot_from, p), piece(slot_to, p), mark(slot_to, p), target)
 
-    for k in hop_order:
+    def to_plane(k):
         target = dev(xor(e, k, experts), xi, ci)
-        for p in range(3):
-            src = out_a.at[k, :, halves[p]] if p < 2 else out_b.at[k]
+        for p in range(2):
+            src = out_b.at[k] if p else out_a.at[k]
             send(src, piece((0, 0, k), p), mark((0, 0, k), p), target)
 
     core_dev = dev(e, xi, lax.rem(ci + 1, gc))
 
     def from_column(k):
-        for p in range(3):
+        for p in range(2):
             if k:
                 arrived((0, 0, k), p)
             for d in range(1, gx):
@@ -296,7 +294,7 @@
             forward((0, 0, k), (1, 0, k), p, core_dev)
 
     def from_chips(k):
-        for p in range(3):
+        for p in range(2):
             for d in range(1, gx):
                 arrived((0, d, k), p)
                 forward((0, d, k), (1, d, k), p, core_dev)
@@ -306,7 +304,7 @@
     tile2 = min(1024, half_width)
 
     def first(k):
-        for d in range(gx):
+        for d in range(0 if k else 1, gx):
             count(cap * width, mark((1, d, k), 0))
         for dc in range(gc):
             for d in range(gx):
@@ -382,37 +380,38 @@
                 for step, k in steps:
                     step(k)
 
-    far = range(2, experts)
+    def do(*steps):
+        for step, k in steps:
+            if k <= last:
+                step(k)
+
+    later = range(4, experts)
+    do((to_plane, 2))
     from_column(0)
+
+    def beside_core(k):
+        count(cap * width, mark((1, 0, k), 0))
+
+    relay(1, [(beside_core, 0), (to_plane, 3), (to_plane, 1)])
     from_chips(0)
-    if last:
-        from_column(1)
-    relay(1, [(from_column, 2)])
+    relay(0, [(to_plane, 3), (to_plane, 1), (beside_core, 0)])
+    do(*[(to_plane, k) for k in later], (from_column, 2))
     first(0)
-    relay(1, [(from_chips, 1), (from_column, 3)])
+    relay(1, [(from_column, 3)])
     second(0)
-    relay(0, [(from_column, k) for k in far] + [(from_chips, 1)])
-    relay(1, [(from_column, k) for k in far if k > 3] + [(from_chips, 2)])
-    if last:
-        first(1)
-    to_chips(0)
-    relay(0, [(from_chips, 2)])
-    for k in far:
-        relay(1, [(from_chips, k + 1)])
-        first(k)
-        relay(0, [(from_chips, k + 1)])
-        if k > 2:
-            to_chips(k - 1)
-        second(k)
-    if last:
-        second(1)
-    if last > 1:
-        to_chips(last)
-    if last:
-        to_chips(1)
-    for k in [*far, *range(min(experts, 2))]:
-        to_column(k)
-
+    relay(0, [(from_column, 3), (from_chips, 2), (from_column, 1)])
+    relay(1, [(from_column, 1), (from_chips, 2)])
+    do((first, 2))
+    relay(1, [(from_chips, 3)])
+    do((second, 2))
+    relay(0, [(from_chips, 3)])
+    relay(1, [(from_chips, 1)])
+    do((to_chips, 2), (to_chips, 0), (first, 3))
+    relay(0, [(from_chips, 1)])
+    do((second, 3), (first, 1), (to_chips, 3), (to_column, 2), (second, 1), (to_chips, 1))
+    for k in later:
+        do((from_column, k), (from_chips, k), (first, k), (second, k), (to_chips, k))
+    do((to_column, 3))
     early[3].wait()
     probs = lax.dot_general(
         normed, router[0], (((1,), (1,)), ((), ())), preferred_element_type=F32
@@ -429,6 +428,7 @@
     high = combine.astype(BF)
     low = (combine - high.astype(F32)).astype(BF)
 
+    do((to_column, 1))
     early[4].wait()
     learner_in = student[0]
     shifted = learner_in - jnp.max(learner_in, axis=-1, keepdims=True)
@@ -438,6 +438,10 @@
     picked = lax.broadcasted_iota(jnp.int32, (tok, vocab), 1).astype(F32) == target_col
     hit = jnp.sum(jnp.where(picked, learner, 0.0), axis=-1, keepdims=True)
     loads[2].wait()
+
+    to_column(0)
+    for k in later:
+        to_column(k)
 
     for h in range(2):
         part = halves[h]
@@ -473,7 +477,7 @@
     @pl.when(is_decoder)
     def _():
         lrecv[mine] = pair
-        for ds in range(n_seg):
+        for ds in reversed(range(n_seg)):
             for d in range(n_exp):
                 if ds or d:
                     pltpu.make_async_remote_copy(
@@ -548,7 +552,7 @@
         v((experts * cap, width), BF), v((experts * rest, width), F32),
         v((1, 128), F32), v(((n_seg - n_seg // 2) * n_exp, 1, 128), F32),
         v((n_seg * n_exp, 1, 128), F32), v((cap * width // 1024, 8, 128), BF),
-        dma((9,)), dma((7,)), dma((2 * blocks,)), dma((blocks,)),
+        dma((9,)), dma((7,)), dma((blocks,)), dma((blocks,)),
         dma((2 * experts,)), dma((2 * nx,)), dma((2 * experts,)),
         dma(()), dma(()), dma(()), pltpu.SemaphoreType.REGULAR((max(experts - 2, 1),)),
     ]

time: 48.7 us -> 48.4 us (level)
  no operation moved by 1% of the time
where the time goes in v4:
time: 48.4 us; the launch traced here: 48.2 us
  Pallas kernels  42.9 us (89%)
  between operations  3.74 us (8%)
  local copies, waits for them, and re-layouts  1.57 us (3%)
    pallas_call x1, Pallas kernels, local(): pl.pallas_call(functools.partial(kernel, n_seg, n_exp, experts, gx, gc),...  42.9 us
    unnamed x1, local copies, waits for them, and re-layouts  1.57 us

profile of v4, /device:TPU:0, one launch (start us, length us, event | category | flops | bytes accessed | tf_op | source)
XLA Modules:
  0.0 48.2 jit_solution(3428942940978262044)
XLA Ops:
  1.9 42.9 %shard_map.131 = (bf16[1,32,2048]{2,1,0:T(8,128)(2,1)}, f32[1,1]{1,0:T(1,128)}) custom-call(bf16[1,32,2048]{2,1,0:T(8,128)(2,1)} %hidden_any.1, bf16[1,32,2048]{2,1,0:T(8,128)(2,1)} %memory.1, s32[1,1]{1,0:T(1,128)S(6)} %copy.16.lengths, s32[1,1]{1,0:T(1,128)S(6)} %copy.17.memory_lengths, s32[1,2,32]{2,1,0:T(2,128)} %bitcast.6, f32[3,1,2048]{2,1,0:T(1,128)} %bitcast.4, ...), custom_call_target="tpu_custom_call" | custom-call | tf_op jit(solution)/shard_map/pallas_call | solution.py:559
  44.8 1.6 %copy.18 = bf16[1,32,2048]{2,1,0:T(8,128)(2,1)} copy(bf16[1,32,2048]{2,1,0:T(8,128)(2,1)} %get-tuple-element.8) | data formatting | bytes 262144

commit v5 on v4

--- a/solution.py
+++ b/solution.py
@@ -103,7 +103,7 @@
     pl.semaphore_wait(barrier, len(near) + beside)
 
     is_decoder = seg >= half_seg
-    groups = 4
+    groups = 2
     band = width // groups
     mem_copies = [
         pltpu.make_async_remote_copy(
@@ -267,7 +267,7 @@
 
     def mark(slot, p):
         if slot[0]:
-            return rb.at[slot[1] * experts + slot[2]]
+            return rb.at[slot[2] + 1 if slot[1] or slot[2] else 0]
         return ra.at[slot[1] * experts + slot[2]]
 
     def arrived(slot, p):
@@ -304,8 +304,7 @@
     tile2 = min(1024, half_width)
 
     def first(k):
-        for d in range(0 if k else 1, gx):
-            count(cap * width, mark((1, d, k), 0))
+        count((gx if k else gx - 1) * cap * width, rb.at[k + 1])
         for dc in range(gc):
             for d in range(gx):
                 stage[d * rest : (d + 1) * rest, :] = x_b[index_b(dc, d, k)].astype(F32)
@@ -551,8 +550,8 @@
         v((experts, main, width), BF), v((experts, rest, width), BF),
         v((experts * cap, width), BF), v((experts * rest, width), F32),
         v((1, 128), F32), v(((n_seg - n_seg // 2) * n_exp, 1, 128), F32),
-        v((n_seg * n_exp, 1, 128), F32), v((cap * width // 1024, 8, 128), BF),
-        dma((9,)), dma((7,)), dma((blocks,)), dma((blocks,)),
+        v((n_seg * n_exp, 1, 128), F32), v((gx * cap * width // 1024, 8, 128), BF),
+        dma((9,)), dma((5,)), dma((blocks,)), dma((experts + 1,)),
         dma((2 * experts,)), dma((2 * nx,)), dma((2 * experts,)),
         dma(()), dma(()), dma(()), pltpu.SemaphoreType.REGULAR((max(experts - 2, 1),)),
     ]

time: 48.4 us -> 48.4 us (level)
  no operation moved by 1% of the time
where the time goes in v5:
time: 48.4 us; the launch traced here: 48.2 us
  Pallas kernels  42.9 us (89%)
  between operations  3.74 us (8%)
  local copies, waits for them, and re-layouts  1.57 us (3%)
    pallas_call x1, Pallas kernels, local(): pl.pallas_call(functools.partial(kernel, n_seg, n_exp, experts, gx, gc),...  42.9 us
    unnamed x1, local copies, waits for them, and re-layouts  1.57 us

profile of v5, /device:TPU:0, one launch (start us, length us, event | category | flops | bytes accessed | tf_op | source)
XLA Modules:
  0.0 48.2 jit_solution(5768798771723943176)
XLA Ops:
  1.9 42.9 %shard_map.131 = (bf16[1,32,2048]{2,1,0:T(8,128)(2,1)}, f32[1,1]{1,0:T(1,128)}) custom-call(bf16[1,32,2048]{2,1,0:T(8,128)(2,1)} %hidden_any.1, bf16[1,32,2048]{2,1,0:T(8,128)(2,1)} %memory.1, s32[1,1]{1,0:T(1,128)S(6)} %copy.16.lengths, s32[1,1]{1,0:T(1,128)S(6)} %copy.17.memory_lengths, s32[1,2,32]{2,1,0:T(2,128)} %bitcast.6, f32[3,1,2048]{2,1,0:T(1,128)} %bitcast.4, ...), custom_call_target="tpu_custom_call" | custom-call | tf_op jit(solution)/shard_map/pallas_call | solution.py:558
  44.8 1.6 %copy.18 = bf16[1,32,2048]{2,1,0:T(8,128)(2,1)} copy(bf16[1,32,2048]{2,1,0:T(8,128)(2,1)} %get-tuple-element.8) | data formatting | bytes 262144
